TPU v7x, 256 devices: a whole 4x4x8 slice. The times are simulated.
256 devices in a mesh: seq: 32 (over y, x, z_hi), head: 8 (over z_lo, core).
Axes of the slice: x: 4, y: 4, z: 8 (z_hi: 2, z_lo: 4; z = z_hi * 4 + z_lo), core: 2. Of those that a mesh axis runs over, the one named last changes fastest.
Arguments:
- queries: bfloat16 [16384, 4096], P(('seq', 'head')), may hold values from -72 to 72
- keys: bfloat16 [16384, 2048], P(('seq', 'head')), may hold values from -6 to 6
- values: bfloat16 [16384, 2048], P(('seq', 'head')), may hold values from -6 to 6
- prefix_keys: bfloat16 [4096, 2048], P(None, 'head'), may hold values from -10 to 10
- prefix_values: bfloat16 [4096, 2048], P(None, 'head'), may hold values from -6 to 6
- span_start: int32 [1], replicated, may hold values from 0 to 4095
Outputs:
- attended: bfloat16 [16384, 4096], P(('seq', 'head'))
All inputs are finite; a program needn't handle non-finite values.
Results may differ from a plain program's by a relative error of at most 0.003.
Values may be sent and summed in bfloat16 or wider, within the bound.
A program may use at most 128 MiB of HBM per device.

v0:
```python
import jax
import jax.numpy as jnp
from jax import lax
from jax.sharding import PartitionSpec as P

HEAD_DIM = 128
QH = 32
KVH = 16
QSCALE = 144
WINDOW = 4096


def shifted(shard, axis, by):
    size = lax.axis_size(axis)
    pairs = [(i, i + by) for i in range(size) if 0 <= i + by < size]
    return lax.ppermute(shard, axis, pairs)


def shortened(shard):
    return jax.tree.map(lambda a: a.astype(jnp.bfloat16) if a.dtype == jnp.float32 else a, shard)


def attend_block(query_rows, key_rows, value_rows, query_first, key_first, start_value):
    block_rows = query_rows.shape[0]
    key_count = key_rows.shape[0]
    grouping = QH // KVH
    scaling = QSCALE ** (-0.5)
    local_groups = key_rows.shape[1] // HEAD_DIM
    query_pos = query_first + jnp.arange(block_rows, dtype=jnp.int32)
    key_pos = key_first + jnp.arange(key_count, dtype=jnp.int32)
    distance = query_pos[:, None] - key_pos[None, :]
    allowed = (distance >= 0) & (distance < WINDOW) & (start_value + key_pos >= 0)[None, :]
    outputs = []
    for key_group in range(local_groups):
        lower = key_group * grouping * HEAD_DIM
        query_head = query_rows[:, lower : lower + grouping * HEAD_DIM].reshape(
            block_rows, grouping, HEAD_DIM
        )
        key_head = key_rows[:, key_group * HEAD_DIM : (key_group + 1) * HEAD_DIM]
        value_head = value_rows[:, key_group * HEAD_DIM : (key_group + 1) * HEAD_DIM]
        scores = (
            jnp.einsum("qgd,kd->gqk", query_head, key_head, preferred_element_type=jnp.float32)
            * scaling
        )
        scores = jnp.where(allowed[None], scores, -jnp.inf)
        peak_score = jnp.max(scores, axis=2, keepdims=True)
        unnormed = jnp.exp(scores - peak_score)
        totals = jnp.sum(unnormed, axis=2)
        weights = unnormed.astype(jnp.bfloat16)
        mixture = jnp.einsum("gqk,kd->qgd", weights, value_head, preferred_element_type=jnp.float32)
        outputs.append(
            (mixture / jnp.transpose(totals)[:, :, None]).reshape(block_rows, grouping * HEAD_DIM)
        )
    return jnp.concatenate(outputs, axis=1).astype(jnp.bfloat16)


def shards(queries, keys, values, prefix_keys, prefix_values, span_start):
    query_local, key_local, value_local = (
        lax.all_to_all(queries, "head", split_axis=1, concat_axis=0, tiled=True),
        lax.all_to_all(keys, "head", split_axis=1, concat_axis=0, tiled=True),
        lax.all_to_all(values, "head", split_axis=1, concat_axis=0, tiled=True),
    )
    seq_rows = query_local.shape[0]
    shards_back = WINDOW // seq_rows
    seq_index = lax.axis_index("seq")

    def relay(step, carried):
        moving_keys, moving_values, window_keys, window_values = carried
        moving_keys, moving_values = shifted((moving_keys, moving_values), "seq", 1)
        offset = (shards_back - 1 - step) * seq_rows
        window_keys = lax.dynamic_update_slice_in_dim(window_keys, moving_keys, offset, 0)
        window_values = lax.dynamic_update_slice_in_dim(window_values, moving_values, offset, 0)
        return (moving_keys, moving_values, window_keys, window_values)

    empty = jnp.zeros((WINDOW, key_local.shape[1]), jnp.bfloat16)
    carried = lax.fori_loop(0, shards_back, relay, (key_local, value_local, empty, empty))
    window_keys = carried[2]
    window_values = carried[3]
    first_row = jnp.minimum(seq_index * seq_rows, WINDOW)
    padded_keys = jnp.concatenate([prefix_keys, jnp.zeros_like(prefix_keys)], axis=0)
    padded_values = jnp.concatenate([prefix_values, jnp.zeros_like(prefix_values)], axis=0)
    window_keys = window_keys + lax.dynamic_slice_in_dim(padded_keys, first_row, WINDOW, 0)
    window_values = window_values + lax.dynamic_slice_in_dim(padded_values, first_row, WINDOW, 0)
    all_keys = jnp.concatenate([window_keys, key_local], axis=0)
    all_values = jnp.concatenate([window_values, value_local], axis=0)
    block_rows = min(512, seq_rows)
    block_count = seq_rows // block_rows
    start_value = span_start[0]
    key_base = (seq_index - shards_back) * seq_rows
    query_base = seq_index * seq_rows

    def one_block(block_index):
        first = block_index * block_rows
        return attend_block(
            query_local, all_keys, all_values, query_base + first, key_base + first, start_value
        )

    blocks = lax.map(one_block, jnp.arange(block_count, dtype=jnp.int32))
    attended = blocks.reshape(seq_rows, query_local.shape[1])
    return lax.all_to_all(
        shortened(attended), "head", split_axis=0, concat_axis=1, tiled=True
    ).astype(attended.dtype)


def solution(mesh):
    placed = (
        P(("seq", "head"), None),
        P(("seq", "head"), None),
        P(("seq", "head"), None),
        P(None, "head"),
        P(None, "head"),
        P(),
    )
    return jax.shard_map(
        shards, mesh=mesh, in_specs=placed, out_specs=P(("seq", "head"), None), check_vma=False
    )
```

profile of v0, /device:TPU:16, one launch (start us, length us, event | category | flops | bytes accessed | tf_op | source)
XLA Modules:
  0.0 381.9 jit_solution(13669239722404619152)
XLA Ops:
  0.0 1.7 copy.73
  1.7 5.9 %all-to-all-start.1 = ((bf16[64,8,256]{2,0,1:T(8,128)(2,1)}), bf16[64,8,256]{2,0,1:T(8,128)(2,1)}, u32[]{:S(2)}, u32[]{:S(2)}) async-start(bf16[64,8,256]{2,0,1:T(8,128)(2,1)} %bitcast.95), calls=%async_computation.1 | async-start | bytes 524288 | tf_op jit(solution)/shard_map/all_to_all | solution.py:61
  8.3 1.7 copy.74
  10.0 7.5 %all-to-all-done.1 = bf16[64,8,256]{2,0,1:T(8,128)(2,1)} async-done(((bf16[64,8,256]{2,0,1:T(8,128)(2,1)}), bf16[64,8,256]{2,0,1:T(8,128)(2,1)}, u32[]{:S(2)}, u32[]{:S(2)}) %all-to-all-start.1) | async-done | bytes 262176 | tf_op jit(solution)/shard_map/all_to_all | solution.py:61
  17.5 3.4 all-to-all-start
  20.9 3.8 %fusion.11 = pred[512,4608]{0,1:T(8,128)(4,1)S(1)} fusion(s32[4608]{0:T(1024)S(1)} %iota_add_fusion, s32[512]{0:T(512)S(1)} %iota_add_fusion.1, pred[4608]{0:T(1024)(128)(4,1)S(1)} %add_compare_fusion), kind=kLoop, calls=%fused_computation.17 | loop fusion | flops 11796480 | bytes 2384384 | tf_op jit(solution)/shard_map/while/body/eval_jaxpr/and | solution.py:32
  24.8 0.8 copy.72
  25.6 4.1 %copy.44 = bf16[4096,256]{0,1:T(8,128)(2,1)} copy(bf16[4096,256]{1,0:T(8,128)(2,1)} %param.12) | data formatting | bytes 4194304 | tf_op args[4]
  29.7 1.8 copy.46
  31.5 5.0 %all-to-all-start.2 = ((bf16[64,8,512]{2,0,1:T(8,128)(2,1)}), bf16[64,8,512]{2,0,1:T(8,128)(2,1)}, u32[]{:S(2)}, u32[]{:S(2)}) async-start(bf16[64,8,512]{2,0,1:T(8,128)(2,1)} %bitcast.94), calls=%async_computation.2 | async-start | bytes 1048576 | tf_op jit(solution)/shard_map/all_to_all | solution.py:59
  37.3 1.6 broadcast.86.clone
  38.8 1.4 broadcast.86
  40.3 204.3 %while.6 = (s32[]{:T(128)}, bf16[512,256]{1,0:T(8,128)(2,1)}, bf16[512,256]{1,0:T(8,128)(2,1)}, bf16[4096,256]{1,0:T(8,128)(2,1)}, bf16[4096,256]{0,1:T(8,128)(2...) while((s32[]{:T(128)}, bf16[512,256]{1,0:T(8,128)(2,1)}, bf16[512,256]{1,0:T(8,128)(2,1)}, ...), condition=%wide.region_1.0_spmd, body=%wide.region_0.0_spmd.sunk | while | flops 7 | bytes 4718839 | solution.py:76
  40.3 7.1 %collective-permute-start.1 = (bf16[512,256]{1,0:T(8,128)(2,1)}, bf16[512,256]{1,0:T(8,128)(2,1)S(1)}, u32[]{:S(2)}, u32[]{:S(2)}) collective-permute-start(bf16[512,256]{1,0:T(8,128)(2,1)} %get-tuple-element.191), channel_id=1, source_target_pairs={{0,8},{8,16},{16,24},{24,32},{32,40},{40,48},{48,56},{56,64},{64,7... | collective-permute-start | bytes 786440 | tf_op jit(solution)/shard_map/while/body/eval_jaxpr/ppermute | solution.py:16
  47.4 3.5 collective-permute-start
  51.0 10.3 %collective-permute-done.1 = bf16[512,256]{1,0:T(8,128)(2,1)S(1)} collective-permute-done((bf16[512,256]{1,0:T(8,128)(2,1)}, bf16[512,256]{1,0:T(8,128)(2,1)S(1)}, u32[]{:S(2)}, u32[]{:S(2)}) %collective-permute-start.1) | collective-permute-done | bytes 262176 | tf_op jit(solution)/shard_map/while/body/eval_jaxpr/ppermute | solution.py:16
  62.1 0.7 constant_dynamic-update-slice_fusion.5
  62.8 6.7 %collective-permute-done = bf16[512,256]{1,0:T(8,128)(2,1)S(1)} collective-permute-done((bf16[512,256]{1,0:T(8,128)(2,1)}, bf16[512,256]{1,0:T(8,128)(2,1)S(1)}, u32[]{:S(2)}, u32[]{:S(2)}) %collective-permute-start) | collective-permute-done | bytes 262176 | tf_op jit(solution)/shard_map/while/body/eval_jaxpr/ppermute | solution.py:16
  71.0 2.6 collective-permute-start.1
  73.6 5.9 %collective-permute-start = (bf16[512,256]{1,0:T(8,128)(2,1)}, bf16[512,256]{1,0:T(8,128)(2,1)S(1)}, u32[]{:S(2)}, u32[]{:S(2)}) collective-permute-start(bf16[512,256]{1,0:T(8,128)(2,1)} %get-tuple-element.190), channel_id=1, source_target_pairs={{0,8},{8,16},{16,24},{24,32},{32,40},{40,48},{48,56},{56,64},{64,7... | collective-permute-start | bytes 786440 | tf_op jit(solution)/shard_map/while/body/eval_jaxpr/ppermute | solution.py:16
  79.6 9.6 %collective-permute-done.1 = bf16[512,256]{1,0:T(8,128)(2,1)S(1)} collective-permute-done((bf16[512,256]{1,0:T(8,128)(2,1)}, bf16[512,256]{1,0:T(8,128)(2,1)S(1)}, u32[]{:S(2)}, u32[]{:S(2)}) %collective-permute-start.1) | collective-permute-done | bytes 262176 | tf_op jit(solution)/shard_map/while/body/eval_jaxpr/ppermute | solution.py:16
  90.0 0.8 constant_dynamic-update-slice_fusion.5
  90.8 3.2 collective-permute-done
  95.5 1.9 collective-permute-start.1
  97.4 4.3 %collective-permute-start = (bf16[512,256]{1,0:T(8,128)(2,1)}, bf16[512,256]{1,0:T(8,128)(2,1)S(1)}, u32[]{:S(2)}, u32[]{:S(2)}) collective-permute-start(bf16[512,256]{1,0:T(8,128)(2,1)} %get-tuple-element.190), channel_id=1, source_target_pairs={{0,8},{8,16},{16,24},{24,32},{32,40},{40,48},{48,56},{56,64},{64,7... | collective-permute-start | bytes 786440 | tf_op jit(solution)/shard_map/while/body/eval_jaxpr/ppermute | solution.py:16
  101.7 12.0 %collective-permute-done.1 = bf16[512,256]{1,0:T(8,128)(2,1)S(1)} collective-permute-done((bf16[512,256]{1,0:T(8,128)(2,1)}, bf16[512,256]{1,0:T(8,128)(2,1)S(1)}, u32[]{:S(2)}, u32[]{:S(2)}) %collective-permute-start.1) | collective-permute-done | bytes 262176 | tf_op jit(solution)/shard_map/while/body/eval_jaxpr/ppermute | solution.py:16
  114.6 0.8 constant_dynamic-update-slice_fusion.5
  115.3 2.3 collective-permute-done
  119.0 1.9 collective-permute-start.1
  120.9 4.8 %collective-permute-start = (bf16[512,256]{1,0:T(8,128)(2,1)}, bf16[512,256]{1,0:T(8,128)(2,1)S(1)}, u32[]{:S(2)}, u32[]{:S(2)}) collective-permute-start(bf16[512,256]{1,0:T(8,128)(2,1)} %get-tuple-element.190), channel_id=1, source_target_pairs={{0,8},{8,16},{16,24},{24,32},{32,40},{40,48},{48,56},{56,64},{64,7... | collective-permute-start | bytes 786440 | tf_op jit(solution)/shard_map/while/body/eval_jaxpr/ppermute | solution.py:16
  125.8 12.2 %collective-permute-done.1 = bf16[512,256]{1,0:T(8,128)(2,1)S(1)} collective-permute-done((bf16[512,256]{1,0:T(8,128)(2,1)}, bf16[512,256]{1,0:T(8,128)(2,1)S(1)}, u32[]{:S(2)}, u32[]{:S(2)}) %collective-permute-start.1) | collective-permute-done | bytes 262176 | tf_op jit(solution)/shard_map/while/body/eval_jaxpr/ppermute | solution.py:16
  138.9 0.8 constant_dynamic-update-slice_fusion.5
  139.6 4.0 %collective-permute-done = bf16[512,256]{1,0:T(8,128)(2,1)S(1)} collective-permute-done((bf16[512,256]{1,0:T(8,128)(2,1)}, bf16[512,256]{1,0:T(8,128)(2,1)S(1)}, u32[]{:S(2)}, u32[]{:S(2)}) %collective-permute-start) | collective-permute-done | bytes 262176 | tf_op jit(solution)/shard_map/while/body/eval_jaxpr/ppermute | solution.py:16
  145.1 1.9 collective-permute-start.1
  147.0 4.5 %collective-permute-start = (bf16[512,256]{1,0:T(8,128)(2,1)}, bf16[512,256]{1,0:T(8,128)(2,1)S(1)}, u32[]{:S(2)}, u32[]{:S(2)}) collective-permute-start(bf16[512,256]{1,0:T(8,128)(2,1)} %get-tuple-element.190), channel_id=1, source_target_pairs={{0,8},{8,16},{16,24},{24,32},{32,40},{40,48},{48,56},{56,64},{64,7... | collective-permute-start | bytes 786440 | tf_op jit(solution)/shard_map/while/body/eval_jaxpr/ppermute | solution.py:16
  151.5 11.7 %collective-permute-done.1 = bf16[512,256]{1,0:T(8,128)(2,1)S(1)} collective-permute-done((bf16[512,256]{1,0:T(8,128)(2,1)}, bf16[512,256]{1,0:T(8,128)(2,1)S(1)}, u32[]{:S(2)}, u32[]{:S(2)}) %collective-permute-start.1) | collective-permute-done | bytes 262176 | tf_op jit(solution)/shard_map/while/body/eval_jaxpr/ppermute | solution.py:16
  164.1 0.8 constant_dynamic-update-slice_fusion.5
  164.8 3.2 collective-permute-done
  169.5 1.9 collective-permute-start.1
  171.4 4.1 %collective-permute-start = (bf16[512,256]{1,0:T(8,128)(2,1)}, bf16[512,256]{1,0:T(8,128)(2,1)S(1)}, u32[]{:S(2)}, u32[]{:S(2)}) collective-permute-start(bf16[512,256]{1,0:T(8,128)(2,1)} %get-tuple-element.190), channel_id=1, source_target_pairs={{0,8},{8,16},{16,24},{24,32},{32,40},{40,48},{48,56},{56,64},{64,7... | collective-permute-start | bytes 786440 | tf_op jit(solution)/shard_map/while/body/eval_jaxpr/ppermute | solution.py:16
  175.5 12.2 %collective-permute-done.1 = bf16[512,256]{1,0:T(8,128)(2,1)S(1)} collective-permute-done((bf16[512,256]{1,0:T(8,128)(2,1)}, bf16[512,256]{1,0:T(8,128)(2,1)S(1)}, u32[]{:S(2)}, u32[]{:S(2)}) %collective-permute-start.1) | collective-permute-done | bytes 262176 | tf_op jit(solution)/shard_map/while/body/eval_jaxpr/ppermute | solution.py:16
  188.6 0.8 constant_dynamic-update-slice_fusion.5
  189.4 4.0 %collective-permute-done = bf16[512,256]{1,0:T(8,128)(2,1)S(1)} collective-permute-done((bf16[512,256]{1,0:T(8,128)(2,1)}, bf16[512,256]{1,0:T(8,128)(2,1)S(1)}, u32[]{:S(2)}, u32[]{:S(2)}) %collective-permute-start) | collective-permute-done | bytes 262176 | tf_op jit(solution)/shard_map/while/body/eval_jaxpr/ppermute | solution.py:16
  194.8 1.9 collective-permute-start.1
  196.7 4.5 %collective-permute-start = (bf16[512,256]{1,0:T(8,128)(2,1)}, bf16[512,256]{1,0:T(8,128)(2,1)S(1)}, u32[]{:S(2)}, u32[]{:S(2)}) collective-permute-start(bf16[512,256]{1,0:T(8,128)(2,1)} %get-tuple-element.190), channel_id=1, source_target_pairs={{0,8},{8,16},{16,24},{24,32},{32,40},{40,48},{48,56},{56,64},{64,7... | collective-permute-start | bytes 786440 | tf_op jit(solution)/shard_map/while/body/eval_jaxpr/ppermute | solution.py:16
  201.2 11.8 %collective-permute-done.1 = bf16[512,256]{1,0:T(8,128)(2,1)S(1)} collective-permute-done((bf16[512,256]{1,0:T(8,128)(2,1)}, bf16[512,256]{1,0:T(8,128)(2,1)S(1)}, u32[]{:S(2)}, u32[]{:S(2)}) %collective-permute-start.1) | collective-permute-done | bytes 262176 | tf_op jit(solution)/shard_map/while/body/eval_jaxpr/ppermute | solution.py:16
  213.8 0.8 constant_dynamic-update-slice_fusion.5
  214.6 3.4 collective-permute-done
  219.4 1.9 collective-permute-start.1
  221.3 3.9 %collective-permute-start = (bf16[512,256]{1,0:T(8,128)(2,1)}, bf16[512,256]{1,0:T(8,128)(2,1)S(1)}, u32[]{:S(2)}, u32[]{:S(2)}) collective-permute-start(bf16[512,256]{1,0:T(8,128)(2,1)} %get-tuple-element.190), channel_id=1, source_target_pairs={{0,8},{8,16},{16,24},{24,32},{32,40},{40,48},{48,56},{56,64},{64,7... | collective-permute-start | bytes 786440 | tf_op jit(solution)/shard_map/while/body/eval_jaxpr/ppermute | solution.py:16
  225.3 12.3 %collective-permute-done.1 = bf16[512,256]{1,0:T(8,128)(2,1)S(1)} collective-permute-done((bf16[512,256]{1,0:T(8,128)(2,1)}, bf16[512,256]{1,0:T(8,128)(2,1)S(1)}, u32[]{:S(2)}, u32[]{:S(2)}) %collective-permute-start.1) | collective-permute-done | bytes 262176 | tf_op jit(solution)/shard_map/while/body/eval_jaxpr/ppermute | solution.py:16
  238.5 0.8 constant_dynamic-update-slice_fusion.5
  239.2 3.9 %collective-permute-done = bf16[512,256]{1,0:T(8,128)(2,1)S(1)} collective-permute-done((bf16[512,256]{1,0:T(8,128)(2,1)}, bf16[512,256]{1,0:T(8,128)(2,1)S(1)}, u32[]{:S(2)}, u32[]{:S(2)}) %collective-permute-start) | collective-permute-done | bytes 262176 | tf_op jit(solution)/shard_map/while/body/eval_jaxpr/ppermute | solution.py:16
  244.5 4.1 %fusion.14 = bf16[4096,256]{0,1:T(8,128)(2,1)} fusion(bf16[4096,256]{0,1:T(8,128)(2,1)} %get-tuple-element.124, s32[]{:T(128)S(6)} %select_n.21, bf16[4096,256]{0,1:T(8,128)(2,1)} %copy.44), kind=kLoop, calls=%fused_computation.26 | loop fusion | flops 4194304 | bytes 6291460 | tf_op jit(solution)/shard_map/add | solution.py:83
  248.6 4.4 %fusion.15 = bf16[4096,256]{1,0:T(8,128)(2,1)} fusion(bf16[4096,256]{1,0:T(8,128)(2,1)S(1)} %copy-done.1, s32[]{:T(128)S(6)} %select_n.21, bf16[4096,256]{1,0:T(8,128)(2,1)S(1)} %copy-done.2), kind=kLoop, calls=%fused_computation.27 | loop fusion | flops 4194304 | bytes 6291460 | tf_op jit(solution)/shard_map/add | solution.py:82
  253.1 1.1 fusion.64
  254.4 9.2 %fusion.4 = (f32[2,512]{1,0:T(2,128)S(1)}, f32[4608,512,2]{1,0,2:T(8,128)}) fusion(pred[512,4608]{0,1:T(8,128)(4,1)S(1)} %fusion.11, bf16[512,2,128]{0,2,1:T(8,128)(2,1)S(1)} %bitcast.106, bf16[4096,256]{1,0:T(8,128)(2,1)} %fusion.15, bf16[512,256]{1,0:T(8,128)(2,1)S(1)} %bitcast.100), kind=kOutput, calls=%fused_computation.10 | convolution fusion | flops 1224473600 | bytes 23859200 | tf_op jit(solution)/shard_map/while/body/eval_jaxpr/qgd,kd->gqk/dot_general | solution.py:42
  263.7 19.0 %fusion = (f32[2,512]{1,0:T(2,128)S(1)}, f32[2,512]{1,0:T(2,128)S(1)}, f32[4608,512,2]{1,0,2:T(8,128)}) fusion(f32[4608,512,2]{1,0,2:T(8,128)} %get-tuple-element.146, f32[2,512]{1,0:T(2,128)S(1)} %get-tuple-element.145, pred[512,4608]{0,1:T(8,128)(4,1)S(1)} %fusion.11, bf16[512,2,128]{0,2,1:T(8,128)(2,1)S(1)} %bitcast.105, ...), kind=kOutput, calls=%fused_computation.6 | convolution fusion | flops 1243346944 | bytes 42741760 | tf_op jit(solution)/shard_map/while/body/eval_jaxpr/qgd,kd->gqk/dot_general | solution.py:42
  282.7 9.8 %fusion.51 = bf16[512,2,128]{0,2,1:T(8,128)(2,1)S(1)} fusion(f32[4608,512,2]{1,0,2:T(8,128)} %get-tuple-element.146, f32[2,512]{1,0:T(2,128)S(1)} %get-tuple-element.145, pred[512,4608]{0,1:T(8,128)(4,1)S(1)} %fusion.11, bf16[4096,256]{0,1:T(8,128)(2,1)S(1)} %copy-done.3, bf16[512,256]{0,1:T(8,128)(2,1)S(1)} %copy-done.6, f32[512,2]{0,1:T(2,128)S(1)} %bitcast.108), kind=kOutput, calls=%fused_computation.45 | convolution fusion | flops 1229455360 | bytes 23863296 | tf_op jit(solution)/shard_map/while/body/eval_jaxpr/gqk,kd->qgd/dot_general | solution.py:50
  292.9 9.9 %fusion.2 = f32[2,512]{1,0:T(2,128)S(1)} fusion(f32[4608,512,2]{1,0,2:T(8,128)} %get-tuple-element.147, f32[2,512]{1,0:T(2,128)S(1)} %get-tuple-element.132, pred[512,4608]{0,1:T(8,128)(4,1)S(1)} %fusion.11), kind=kLoop, calls=%fused_computation.8 | loop fusion | flops 18873344 | bytes 21241856 | tf_op jit(solution)/shard_map/while/body/eval_jaxpr/reduce_sum | solution.py:48
  302.7 1.9 copy-done
  304.7 6.9 %fusion.41 = bf16[512,2,128]{0,2,1:T(8,128)(2,1)S(1)} fusion(f32[4608,512,2]{1,0,2:T(8,128)S(1)} %copy-done, f32[2,512]{1,0:T(2,128)S(1)} %get-tuple-element.132, pred[512,4608]{0,1:T(8,128)(4,1)S(1)} %fusion.11, bf16[512,256]{0,1:T(8,128)(2,1)S(1)} %copy-done.6, bf16[4096,256]{0,1:T(8,128)(2,1)} %fusion.14, f32[512,2]{0,1:T(2,128)S(1)} %bitcast.107), kind=kOutput, calls=%fused_computation.43 | convolution fusion | flops 1229455360 | bytes 23863296 | tf_op jit(solution)/shard_map/while/body/eval_jaxpr/gqk,kd->qgd/dot_general | solution.py:50
  312.0 69.0 %all_to_all.73 = bf16[8,64,512]{2,1,0:T(8,128)(2,1)S(1)} all-to-all(bf16[8,64,512]{2,1,0:T(8,128)(2,1)S(1)} %pad_maximum_fusion.2), channel_id=1, replica_groups=mesh['seq'=32,'head'=8] {'head'}, dimensions={0} | all-to-all | bytes 1048576 | tf_op jit(solution)/shard_map/all_to_all | solution.py:100
  381.0 0.8 copy.68
  (58 shorter events, 19.9 us)
Async XLA Ops:
  0.0 24.8 %copy-start.5 = (bf16[64,4096]{1,0:T(8,128)(2,1)S(1)}, bf16[64,4096]{1,0:T(8,128)(2,1)}, u32[]{:S(2)}) copy-start(bf16[64,4096]{1,0:T(8,128)(2,1)} %param.8) | copy-start | bytes 1572868
  1.7 15.8 %all-to-all-start.1 = ((bf16[64,8,256]{2,0,1:T(8,128)(2,1)}), bf16[64,8,256]{2,0,1:T(8,128)(2,1)}, u32[]{:S(2)}, u32[]{:S(2)}) async-start(bf16[64,8,256]{2,0,1:T(8,128)(2,1)} %bitcast.95), calls=%async_computation.1 | async-start | bytes 524288 | tf_op jit(solution)/shard_map/all_to_all | solution.py:61
  17.5 14.1 %all-to-all-start = ((bf16[64,8,256]{2,0,1:T(8,128)(2,1)}), bf16[64,8,256]{2,0,1:T(8,128)(2,1)S(1)}, u32[]{:S(2)}, u32[]{:S(2)}) async-start(bf16[64,8,256]{2,0,1:T(8,128)(2,1)} %bitcast.96), calls=%async_computation | async-start | bytes 524288 | tf_op jit(solution)/shard_map/all_to_all | solution.py:60
  31.5 221.5 %all-to-all-start.2 = ((bf16[64,8,512]{2,0,1:T(8,128)(2,1)}), bf16[64,8,512]{2,0,1:T(8,128)(2,1)}, u32[]{:S(2)}, u32[]{:S(2)}) async-start(bf16[64,8,512]{2,0,1:T(8,128)(2,1)} %bitcast.94), calls=%async_computation.2 | async-start | bytes 1048576 | tf_op jit(solution)/shard_map/all_to_all | solution.py:59
  40.3 21.0 %collective-permute-start.1 = (bf16[512,256]{1,0:T(8,128)(2,1)}, bf16[512,256]{1,0:T(8,128)(2,1)S(1)}, u32[]{:S(2)}, u32[]{:S(2)}) collective-permute-start(bf16[512,256]{1,0:T(8,128)(2,1)} %get-tuple-element.191), channel_id=1, source_target_pairs={{0,8},{8,16},{16,24},{24,32},{32,40},{40,48},{48,56},{56,64},{64,7... | collective-permute-start | bytes 786440 | tf_op jit(solution)/shard_map/while/body/eval_jaxpr/ppermute | solution.py:16
  47.4 22.2 %collective-permute-start = (bf16[512,256]{1,0:T(8,128)(2,1)}, bf16[512,256]{1,0:T(8,128)(2,1)S(1)}, u32[]{:S(2)}, u32[]{:S(2)}) collective-permute-start(bf16[512,256]{1,0:T(8,128)(2,1)} %get-tuple-element.190), channel_id=1, source_target_pairs={{0,8},{8,16},{16,24},{24,32},{32,40},{40,48},{48,56},{56,64},{64,7... | collective-permute-start | bytes 786440 | tf_op jit(solution)/shard_map/while/body/eval_jaxpr/ppermute | solution.py:16
  71.0 18.2 %collective-permute-start.1 = (bf16[512,256]{1,0:T(8,128)(2,1)}, bf16[512,256]{1,0:T(8,128)(2,1)S(1)}, u32[]{:S(2)}, u32[]{:S(2)}) collective-permute-start(bf16[512,256]{1,0:T(8,128)(2,1)} %get-tuple-element.191), channel_id=1, source_target_pairs={{0,8},{8,16},{16,24},{24,32},{32,40},{40,48},{48,56},{56,64},{64,7... | collective-permute-start | bytes 786440 | tf_op jit(solution)/shard_map/while/body/eval_jaxpr/ppermute | solution.py:16
  73.6 20.4 %collective-permute-start = (bf16[512,256]{1,0:T(8,128)(2,1)}, bf16[512,256]{1,0:T(8,128)(2,1)S(1)}, u32[]{:S(2)}, u32[]{:S(2)}) collective-permute-start(bf16[512,256]{1,0:T(8,128)(2,1)} %get-tuple-element.190), channel_id=1, source_target_pairs={{0,8},{8,16},{16,24},{24,32},{32,40},{40,48},{48,56},{56,64},{64,7... | collective-permute-start | bytes 786440 | tf_op jit(solution)/shard_map/while/body/eval_jaxpr/ppermute | solution.py:16
  95.5 18.3 %collective-permute-start.1 = (bf16[512,256]{1,0:T(8,128)(2,1)}, bf16[512,256]{1,0:T(8,128)(2,1)S(1)}, u32[]{:S(2)}, u32[]{:S(2)}) collective-permute-start(bf16[512,256]{1,0:T(8,128)(2,1)} %get-tuple-element.191), channel_id=1, source_target_pairs={{0,8},{8,16},{16,24},{24,32},{32,40},{40,48},{48,56},{56,64},{64,7... | collective-permute-start | bytes 786440 | tf_op jit(solution)/shard_map/while/body/eval_jaxpr/ppermute | solution.py:16
  97.4 20.2 %collective-permute-start = (bf16[512,256]{1,0:T(8,128)(2,1)}, bf16[512,256]{1,0:T(8,128)(2,1)S(1)}, u32[]{:S(2)}, u32[]{:S(2)}) collective-permute-start(bf16[512,256]{1,0:T(8,128)(2,1)} %get-tuple-element.190), channel_id=1, source_target_pairs={{0,8},{8,16},{16,24},{24,32},{32,40},{40,48},{48,56},{56,64},{64,7... | collective-permute-start | bytes 786440 | tf_op jit(solution)/shard_map/while/body/eval_jaxpr/ppermute | solution.py:16
  119.0 19.0 %collective-permute-start.1 = (bf16[512,256]{1,0:T(8,128)(2,1)}, bf16[512,256]{1,0:T(8,128)(2,1)S(1)}, u32[]{:S(2)}, u32[]{:S(2)}) collective-permute-start(bf16[512,256]{1,0:T(8,128)(2,1)} %get-tuple-element.191), channel_id=1, source_target_pairs={{0,8},{8,16},{16,24},{24,32},{32,40},{40,48},{48,56},{56,64},{64,7... | collective-permute-start | bytes 786440 | tf_op jit(solution)/shard_map/while/body/eval_jaxpr/ppermute | solution.py:16
  120.9 22.7 %collective-permute-start = (bf16[512,256]{1,0:T(8,128)(2,1)}, bf16[512,256]{1,0:T(8,128)(2,1)S(1)}, u32[]{:S(2)}, u32[]{:S(2)}) collective-permute-start(bf16[512,256]{1,0:T(8,128)(2,1)} %get-tuple-element.190), channel_id=1, source_target_pairs={{0,8},{8,16},{16,24},{24,32},{32,40},{40,48},{48,56},{56,64},{64,7... | collective-permute-start | bytes 786440 | tf_op jit(solution)/shard_map/while/body/eval_jaxpr/ppermute | solution.py:16
  145.1 18.2 %collective-permute-start.1 = (bf16[512,256]{1,0:T(8,128)(2,1)}, bf16[512,256]{1,0:T(8,128)(2,1)S(1)}, u32[]{:S(2)}, u32[]{:S(2)}) collective-permute-start(bf16[512,256]{1,0:T(8,128)(2,1)} %get-tuple-element.191), channel_id=1, source_target_pairs={{0,8},{8,16},{16,24},{24,32},{32,40},{40,48},{48,56},{56,64},{64,7... | collective-permute-start | bytes 786440 | tf_op jit(solution)/shard_map/while/body/eval_jaxpr/ppermute | solution.py:16
  147.0 21.1 %collective-permute-start = (bf16[512,256]{1,0:T(8,128)(2,1)}, bf16[512,256]{1,0:T(8,128)(2,1)S(1)}, u32[]{:S(2)}, u32[]{:S(2)}) collective-permute-start(bf16[512,256]{1,0:T(8,128)(2,1)} %get-tuple-element.190), channel_id=1, source_target_pairs={{0,8},{8,16},{16,24},{24,32},{32,40},{40,48},{48,56},{56,64},{64,7... | collective-permute-start | bytes 786440 | tf_op jit(solution)/shard_map/while/body/eval_jaxpr/ppermute | solution.py:16
  169.5 18.3 %collective-permute-start.1 = (bf16[512,256]{1,0:T(8,128)(2,1)}, bf16[512,256]{1,0:T(8,128)(2,1)S(1)}, u32[]{:S(2)}, u32[]{:S(2)}) collective-permute-start(bf16[512,256]{1,0:T(8,128)(2,1)} %get-tuple-element.191), channel_id=1, source_target_pairs={{0,8},{8,16},{16,24},{24,32},{32,40},{40,48},{48,56},{56,64},{64,7... | collective-permute-start | bytes 786440 | tf_op jit(solution)/shard_map/while/body/eval_jaxpr/ppermute | solution.py:16
  171.4 22.0 %collective-permute-start = (bf16[512,256]{1,0:T(8,128)(2,1)}, bf16[512,256]{1,0:T(8,128)(2,1)S(1)}, u32[]{:S(2)}, u32[]{:S(2)}) collective-permute-start(bf16[512,256]{1,0:T(8,128)(2,1)} %get-tuple-element.190), channel_id=1, source_target_pairs={{0,8},{8,16},{16,24},{24,32},{32,40},{40,48},{48,56},{56,64},{64,7... | collective-permute-start | bytes 786440 | tf_op jit(solution)/shard_map/while/body/eval_jaxpr/ppermute | solution.py:16
  194.8 18.2 %collective-permute-start.1 = (bf16[512,256]{1,0:T(8,128)(2,1)}, bf16[512,256]{1,0:T(8,128)(2,1)S(1)}, u32[]{:S(2)}, u32[]{:S(2)}) collective-permute-start(bf16[512,256]{1,0:T(8,128)(2,1)} %get-tuple-element.191), channel_id=1, source_target_pairs={{0,8},{8,16},{16,24},{24,32},{32,40},{40,48},{48,56},{56,64},{64,7... | collective-permute-start | bytes 786440 | tf_op jit(solution)/shard_map/while/body/eval_jaxpr/ppermute | solution.py:16
  196.7 21.3 %collective-permute-start = (bf16[512,256]{1,0:T(8,128)(2,1)}, bf16[512,256]{1,0:T(8,128)(2,1)S(1)}, u32[]{:S(2)}, u32[]{:S(2)}) collective-permute-start(bf16[512,256]{1,0:T(8,128)(2,1)} %get-tuple-element.190), channel_id=1, source_target_pairs={{0,8},{8,16},{16,24},{24,32},{32,40},{40,48},{48,56},{56,64},{64,7... | collective-permute-start | bytes 786440 | tf_op jit(solution)/shard_map/while/body/eval_jaxpr/ppermute | solution.py:16
  219.4 18.2 %collective-permute-start.1 = (bf16[512,256]{1,0:T(8,128)(2,1)}, bf16[512,256]{1,0:T(8,128)(2,1)S(1)}, u32[]{:S(2)}, u32[]{:S(2)}) collective-permute-start(bf16[512,256]{1,0:T(8,128)(2,1)} %get-tuple-element.191), channel_id=1, source_target_pairs={{0,8},{8,16},{16,24},{24,32},{32,40},{40,48},{48,56},{56,64},{64,7... | collective-permute-start | bytes 786440 | tf_op jit(solution)/shard_map/while/body/eval_jaxpr/ppermute | solution.py:16
  221.3 21.8 %collective-permute-start = (bf16[512,256]{1,0:T(8,128)(2,1)}, bf16[512,256]{1,0:T(8,128)(2,1)S(1)}, u32[]{:S(2)}, u32[]{:S(2)}) collective-permute-start(bf16[512,256]{1,0:T(8,128)(2,1)} %get-tuple-element.190), channel_id=1, source_target_pairs={{0,8},{8,16},{16,24},{24,32},{32,40},{40,48},{48,56},{56,64},{64,7... | collective-permute-start | bytes 786440 | tf_op jit(solution)/shard_map/while/body/eval_jaxpr/ppermute | solution.py:16
  244.5 4.1 %copy-start.1 = (bf16[4096,256]{1,0:T(8,128)(2,1)S(1)}, bf16[4096,256]{1,0:T(8,128)(2,1)}, u32[]{:S(2)}) copy-start(bf16[4096,256]{1,0:T(8,128)(2,1)} %get-tuple-element.125) | copy-start | bytes 6291460
  244.5 4.1 %copy-start.2 = (bf16[4096,256]{1,0:T(8,128)(2,1)S(1)}, bf16[4096,256]{1,0:T(8,128)(2,1)}, u32[]{:S(2)}) copy-start(bf16[4096,256]{1,0:T(8,128)(2,1)} %param.11) | copy-start | bytes 6291460
  254.4 9.3 %copy-start.4 = (bf16[4096,256]{1,0:T(8,128)(2,1)S(1)}, bf16[4096,256]{1,0:T(8,128)(2,1)}, u32[]{:S(2)}) copy-start(bf16[4096,256]{1,0:T(8,128)(2,1)} %fusion.15) | copy-start | bytes 6291460
  263.7 19.0 %copy-start.3 = (bf16[4096,256]{0,1:T(8,128)(2,1)S(1)}, bf16[4096,256]{0,1:T(8,128)(2,1)}, u32[]{:S(2)}) copy-start(bf16[4096,256]{0,1:T(8,128)(2,1)} %fusion.14) | copy-start | bytes 6291460
  263.7 19.0 %copy-start.6 = (bf16[512,256]{0,1:T(8,128)(2,1)S(1)}, bf16[512,256]{0,1:T(8,128)(2,1)}, u32[]{:S(2)}) copy-start(bf16[512,256]{0,1:T(8,128)(2,1)} %copy.46) | copy-start | bytes 786436
  292.9 11.8 %copy-start = (f32[4608,512,2]{1,0,2:T(8,128)S(1)}, f32[4608,512,2]{1,0,2:T(8,128)}, u32[]{:S(2)}) copy-start(f32[4608,512,2]{1,0,2:T(8,128)} %get-tuple-element.147) | copy-start | bytes 56623108
where the time goes:
time: 383 us; the launch traced here: 382 us
  waiting for transfers between devices  130 us (34%)
  starting transfers between devices  71.2 us (19%)
  blocking collectives  69 us (18%)
  matrix products  45 us (12%)
  local copies, waits for them, and re-layouts  42.9 us (11%)
  other arithmetic  22.3 us (6%)
    ppermute x16, waiting for transfers between devices, shifted(): return lax.ppermute(shard, axis, pairs)  123 us
    all_to_all x1, blocking collectives, shards(): lax.all_to_all(shortened(attended), 'head', split_axis=0, concat_axis=1,...  69 us
    ppermute x16, starting transfers between devices, shifted(): return lax.ppermute(shard, axis, pairs)  56.9 us
    dot_general x2, matrix products, attend_block(): jnp.einsum('qgd,kd->gqk', query_head, key_head, preferred_element_type=jn...  28.2 us
    dot_general x2, matrix products, attend_block(): jnp.einsum('gqk,kd->qgd', weights, value_head, preferred_element_type=jnp...  16.8 us
    while x16, local copies, waits for them, and re-layouts  11.3 us
    reduce_sum x1, other arithmetic, attend_block(): totals = jnp.sum(unnormed, axis=2)  9.86 us
  transfers between devices with their start and end apart: 19, of which 17 were waited for; matrix products, arithmetic and copies ran while one was open for 13% of the time, Pallas kernels for 0%

commit v1 on v0

--- a/solution.py
+++ b/solution.py
@@ -2,12 +2,25 @@
 import jax.numpy as jnp
 from jax import lax
 from jax.sharding import PartitionSpec as P
+from jax.lax import all_to_all, axis_size
 
 HEAD_DIM = 128
 QH = 32
 KVH = 16
 QSCALE = 144
 WINDOW = 4096
+
+
+def play_plane_up(mesh_name, arr_in):
+    return jnp.concatenate(
+        all_to_all(
+            jnp.stack(jnp.split(arr_in, axis_size(mesh_name), axis=1)),
+            mesh_name,
+            split_axis=0,
+            concat_axis=0,
+        ),
+        0,
+    )
 
 
 def shifted(shard, axis, by):
@@ -58,7 +71,7 @@
     query_local, key_local, value_local = (
         lax.all_to_all(queries, "head", split_axis=1, concat_axis=0, tiled=True),
         lax.all_to_all(keys, "head", split_axis=1, concat_axis=0, tiled=True),
-        lax.all_to_all(values, "head", split_axis=1, concat_axis=0, tiled=True),
+        play_plane_up("head", values),
     )
     seq_rows = query_local.shape[0]
     shards_back = WINDOW // seq_rows

time: 383 us -> 393 us (1.026)
  local copies, waits for them, and re-layouts: 42.9 us -> 52.3 us
    unnamed x16 -> x23, local copies, waits for them, and re-layouts: 6.78 us -> 16.5 us
  transfers between devices with their start and end apart: 19 -> 19, of which waited for: 17 -> 17; matrix products, arithmetic and copies ran while one was open for 13% -> 12% of each run, Pallas kernels for 0% -> 0%
where the time goes in v1:
time: 393 us; the launch traced here: 391 us
  waiting for transfers between devices  130 us (33%)
  starting transfers between devices  71.2 us (18%)
  blocking collectives  69 us (18%)
  local copies, waits for them, and re-layouts  52.3 us (13%)
  matrix products  45 us (11%)
  other arithmetic  22.3 us (6%)
    ppermute x16, waiting for transfers between devices, shifted(): return lax.ppermute(shard, axis, pairs)  123 us
    all_to_all x1, blocking collectives, shards(): lax.all_to_all(shortened(attended), 'head', split_axis=0, concat_axis=1,...  69 us
    ppermute x16, starting transfers between devices, shifted(): return lax.ppermute(shard, axis, pairs)  56.9 us
    dot_general x2, matrix products, attend_block(): jnp.einsum('qgd,kd->gqk', query_head, key_head, preferred_element_type=jn...  28.2 us
    dot_general x2, matrix products, attend_block(): jnp.einsum('gqk,kd->qgd', weights, value_head, preferred_element_type=jnp...  16.8 us
    unnamed x23, local copies, waits for them, and re-layouts  16.5 us
    while x16, local copies, waits for them, and re-layouts  11.3 us
    reduce_sum x1, other arithmetic, attend_block(): totals = jnp.sum(unnormed, axis=2)  9.86 us
  transfers between devices with their start and end apart: 19, of which 17 were waited for; matrix products, arithmetic and copies ran while one was open for 12% of the time, Pallas kernels for 0%

profile of v1, /device:TPU:16, one launch (start us, length us, event | category | flops | bytes accessed | tf_op | source)
XLA Modules:
  0.0 391.2 jit_solution(9928690206103628419)
XLA Ops:
  0.0 1.4 bitcast_dynamic-update-slice_fusion.7
  1.4 1.4 bitcast_dynamic-update-slice_fusion.6
  2.8 1.4 bitcast_dynamic-update-slice_fusion.5
  4.2 1.4 bitcast_dynamic-update-slice_fusion.4
  5.6 1.4 bitcast_dynamic-update-slice_fusion.3
  6.9 1.4 bitcast_dynamic-update-slice_fusion.2
  8.3 1.4 bitcast_dynamic-update-slice_fusion.1
  9.7 1.4 bitcast_dynamic-update-slice_fusion
  11.1 5.9 %all-to-all-start.1 = ((bf16[8,64,256]{2,1,0:T(8,128)(2,1)}), bf16[8,64,256]{2,1,0:T(8,128)(2,1)}, u32[]{:S(2)}, u32[]{:S(2)}) async-start(bf16[8,64,256]{2,1,0:T(8,128)(2,1)} %bitcast_dynamic-update-slice_fusion), calls=%async_computation.1 | async-start | bytes 524288 | tf_op jit(solution)/shard_map/all_to_all | solution.py:16
  17.6 1.7 copy.69
  19.3 7.5 %all-to-all-done.1 = bf16[8,64,256]{2,1,0:T(8,128)(2,1)} async-done(((bf16[8,64,256]{2,1,0:T(8,128)(2,1)}), bf16[8,64,256]{2,1,0:T(8,128)(2,1)}, u32[]{:S(2)}, u32[]{:S(2)}) %all-to-all-start.1) | async-done | bytes 262176 | tf_op jit(solution)/shard_map/all_to_all | solution.py:16
  26.8 3.4 all-to-all-start
  30.2 3.8 fusion.11
  34.1 0.8 copy.68
  34.9 4.1 %copy.42 = bf16[4096,256]{0,1:T(8,128)(2,1)} copy(bf16[4096,256]{1,0:T(8,128)(2,1)} %param.12) | data formatting | bytes 4194304 | tf_op args[4]
  39.1 1.8 copy.44
  40.9 5.0 %all-to-all-start.2 = ((bf16[64,8,512]{2,0,1:T(8,128)(2,1)}), bf16[64,8,512]{2,0,1:T(8,128)(2,1)}, u32[]{:S(2)}, u32[]{:S(2)}) async-start(bf16[64,8,512]{2,0,1:T(8,128)(2,1)} %bitcast.105), calls=%async_computation.2 | async-start | bytes 1048576 | tf_op jit(solution)/shard_map/all_to_all | solution.py:72
  46.6 1.6 broadcast.86.clone
  48.2 1.4 broadcast.86
  49.6 204.3 %while.6 = (s32[]{:T(128)}, bf16[512,256]{1,0:T(8,128)(2,1)}, bf16[512,256]{1,0:T(8,128)(2,1)}, bf16[4096,256]{1,0:T(8,128)(2,1)}, bf16[4096,256]{0,1:T(8,128)(2...) while((s32[]{:T(128)}, bf16[512,256]{1,0:T(8,128)(2,1)}, bf16[512,256]{1,0:T(8,128)(2,1)}, ...), condition=%wide.region_1.0_spmd, body=%wide.region_0.0_spmd.sunk | while | flops 7 | bytes 4718839 | solution.py:89
  49.6 7.1 %collective-permute-start.1 = (bf16[512,256]{1,0:T(8,128)(2,1)}, bf16[512,256]{1,0:T(8,128)(2,1)S(1)}, u32[]{:S(2)}, u32[]{:S(2)}) collective-permute-start(bf16[512,256]{1,0:T(8,128)(2,1)} %get-tuple-element.191), channel_id=1, source_target_pairs={{0,8},{8,16},{16,24},{24,32},{32,40},{40,48},{48,56},{56,64},{64,7... | collective-permute-start | bytes 786440 | tf_op jit(solution)/shard_map/while/body/eval_jaxpr/ppermute | solution.py:29
  56.7 3.5 collective-permute-start
  60.3 10.3 %collective-permute-done.1 = bf16[512,256]{1,0:T(8,128)(2,1)S(1)} collective-permute-done((bf16[512,256]{1,0:T(8,128)(2,1)}, bf16[512,256]{1,0:T(8,128)(2,1)S(1)}, u32[]{:S(2)}, u32[]{:S(2)}) %collective-permute-start.1) | collective-permute-done | bytes 262176 | tf_op jit(solution)/shard_map/while/body/eval_jaxpr/ppermute | solution.py:29
  72.2 6.7 %collective-permute-done = bf16[512,256]{1,0:T(8,128)(2,1)S(1)} collective-permute-done((bf16[512,256]{1,0:T(8,128)(2,1)}, bf16[512,256]{1,0:T(8,128)(2,1)S(1)}, u32[]{:S(2)}, u32[]{:S(2)}) %collective-permute-start) | collective-permute-done | bytes 262176 | tf_op jit(solution)/shard_map/while/body/eval_jaxpr/ppermute | solution.py:29
  80.3 2.6 collective-permute-start.1
  82.9 5.9 %collective-permute-start = (bf16[512,256]{1,0:T(8,128)(2,1)}, bf16[512,256]{1,0:T(8,128)(2,1)S(1)}, u32[]{:S(2)}, u32[]{:S(2)}) collective-permute-start(bf16[512,256]{1,0:T(8,128)(2,1)} %get-tuple-element.190), channel_id=1, source_target_pairs={{0,8},{8,16},{16,24},{24,32},{32,40},{40,48},{48,56},{56,64},{64,7... | collective-permute-start | bytes 786440 | tf_op jit(solution)/shard_map/while/body/eval_jaxpr/ppermute | solution.py:29
  88.9 9.6 %collective-permute-done.1 = bf16[512,256]{1,0:T(8,128)(2,1)S(1)} collective-permute-done((bf16[512,256]{1,0:T(8,128)(2,1)}, bf16[512,256]{1,0:T(8,128)(2,1)S(1)}, u32[]{:S(2)}, u32[]{:S(2)}) %collective-permute-start.1) | collective-permute-done | bytes 262176 | tf_op jit(solution)/shard_map/while/body/eval_jaxpr/ppermute | solution.py:29
  99.4 0.8 constant_dynamic-update-slice_fusion.5
  100.1 3.2 collective-permute-done
  104.8 1.9 collective-permute-start.1
  106.7 4.3 %collective-permute-start = (bf16[512,256]{1,0:T(8,128)(2,1)}, bf16[512,256]{1,0:T(8,128)(2,1)S(1)}, u32[]{:S(2)}, u32[]{:S(2)}) collective-permute-start(bf16[512,256]{1,0:T(8,128)(2,1)} %get-tuple-element.190), channel_id=1, source_target_pairs={{0,8},{8,16},{16,24},{24,32},{32,40},{40,48},{48,56},{56,64},{64,7... | collective-permute-start | bytes 786440 | tf_op jit(solution)/shard_map/while/body/eval_jaxpr/ppermute | solution.py:29
  111.1 12.0 %collective-permute-done.1 = bf16[512,256]{1,0:T(8,128)(2,1)S(1)} collective-permute-done((bf16[512,256]{1,0:T(8,128)(2,1)}, bf16[512,256]{1,0:T(8,128)(2,1)S(1)}, u32[]{:S(2)}, u32[]{:S(2)}) %collective-permute-start.1) | collective-permute-done | bytes 262176 | tf_op jit(solution)/shard_map/while/body/eval_jaxpr/ppermute | solution.py:29
  124.7 2.3 collective-permute-done
  128.3 1.9 collective-permute-start.1
  130.3 4.8 %collective-permute-start = (bf16[512,256]{1,0:T(8,128)(2,1)}, bf16[512,256]{1,0:T(8,128)(2,1)S(1)}, u32[]{:S(2)}, u32[]{:S(2)}) collective-permute-start(bf16[512,256]{1,0:T(8,128)(2,1)} %get-tuple-element.190), channel_id=1, source_target_pairs={{0,8},{8,16},{16,24},{24,32},{32,40},{40,48},{48,56},{56,64},{64,7... | collective-permute-start | bytes 786440 | tf_op jit(solution)/shard_map/while/body/eval_jaxpr/ppermute | solution.py:29
  135.1 12.2 %collective-permute-done.1 = bf16[512,256]{1,0:T(8,128)(2,1)S(1)} collective-permute-done((bf16[512,256]{1,0:T(8,128)(2,1)}, bf16[512,256]{1,0:T(8,128)(2,1)S(1)}, u32[]{:S(2)}, u32[]{:S(2)}) %collective-permute-start.1) | collective-permute-done | bytes 262176 | tf_op jit(solution)/shard_map/while/body/eval_jaxpr/ppermute | solution.py:29
  148.9 4.0 %collective-permute-done = bf16[512,256]{1,0:T(8,128)(2,1)S(1)} collective-permute-done((bf16[512,256]{1,0:T(8,128)(2,1)}, bf16[512,256]{1,0:T(8,128)(2,1)S(1)}, u32[]{:S(2)}, u32[]{:S(2)}) %collective-permute-start) | collective-permute-done | bytes 262176 | tf_op jit(solution)/shard_map/while/body/eval_jaxpr/ppermute | solution.py:29
  154.4 1.9 collective-permute-start.1
  156.3 4.5 %collective-permute-start = (bf16[512,256]{1,0:T(8,128)(2,1)}, bf16[512,256]{1,0:T(8,128)(2,1)S(1)}, u32[]{:S(2)}, u32[]{:S(2)}) collective-permute-start(bf16[512,256]{1,0:T(8,128)(2,1)} %get-tuple-element.190), channel_id=1, source_target_pairs={{0,8},{8,16},{16,24},{24,32},{32,40},{40,48},{48,56},{56,64},{64,7... | collective-permute-start | bytes 786440 | tf_op jit(solution)/shard_map/while/body/eval_jaxpr/ppermute | solution.py:29
  160.8 11.7 %collective-permute-done.1 = bf16[512,256]{1,0:T(8,128)(2,1)S(1)} collective-permute-done((bf16[512,256]{1,0:T(8,128)(2,1)}, bf16[512,256]{1,0:T(8,128)(2,1)S(1)}, u32[]{:S(2)}, u32[]{:S(2)}) %collective-permute-start.1) | collective-permute-done | bytes 262176 | tf_op jit(solution)/shard_map/while/body/eval_jaxpr/ppermute | solution.py:29
  174.2 3.2 collective-permute-done
  178.8 1.9 collective-permute-start.1
  180.7 4.1 %collective-permute-start = (bf16[512,256]{1,0:T(8,128)(2,1)}, bf16[512,256]{1,0:T(8,128)(2,1)S(1)}, u32[]{:S(2)}, u32[]{:S(2)}) collective-permute-start(bf16[512,256]{1,0:T(8,128)(2,1)} %get-tuple-element.190), channel_id=1, source_target_pairs={{0,8},{8,16},{16,24},{24,32},{32,40},{40,48},{48,56},{56,64},{64,7... | collective-permute-start | bytes 786440 | tf_op jit(solution)/shard_map/while/body/eval_jaxpr/ppermute | solution.py:29
  184.9 12.2 %collective-permute-done.1 = bf16[512,256]{1,0:T(8,128)(2,1)S(1)} collective-permute-done((bf16[512,256]{1,0:T(8,128)(2,1)}, bf16[512,256]{1,0:T(8,128)(2,1)S(1)}, u32[]{:S(2)}, u32[]{:S(2)}) %collective-permute-start.1) | collective-permute-done | bytes 262176 | tf_op jit(solution)/shard_map/while/body/eval_jaxpr/ppermute | solution.py:29
  198.7 4.0 %collective-permute-done = bf16[512,256]{1,0:T(8,128)(2,1)S(1)} collective-permute-done((bf16[512,256]{1,0:T(8,128)(2,1)}, bf16[512,256]{1,0:T(8,128)(2,1)S(1)}, u32[]{:S(2)}, u32[]{:S(2)}) %collective-permute-start) | collective-permute-done | bytes 262176 | tf_op jit(solution)/shard_map/while/body/eval_jaxpr/ppermute | solution.py:29
  204.1 1.9 collective-permute-start.1
  206.0 4.5 %collective-permute-start = (bf16[512,256]{1,0:T(8,128)(2,1)}, bf16[512,256]{1,0:T(8,128)(2,1)S(1)}, u32[]{:S(2)}, u32[]{:S(2)}) collective-permute-start(bf16[512,256]{1,0:T(8,128)(2,1)} %get-tuple-element.190), channel_id=1, source_target_pairs={{0,8},{8,16},{16,24},{24,32},{32,40},{40,48},{48,56},{56,64},{64,7... | collective-permute-start | bytes 786440 | tf_op jit(solution)/shard_map/while/body/eval_jaxpr/ppermute | solution.py:29
  210.5 11.8 %collective-permute-done.1 = bf16[512,256]{1,0:T(8,128)(2,1)S(1)} collective-permute-done((bf16[512,256]{1,0:T(8,128)(2,1)}, bf16[512,256]{1,0:T(8,128)(2,1)S(1)}, u32[]{:S(2)}, u32[]{:S(2)}) %collective-permute-start.1) | collective-permute-done | bytes 262176 | tf_op jit(solution)/shard_map/while/body/eval_jaxpr/ppermute | solution.py:29
  223.9 3.4 collective-permute-done
  228.7 1.9 collective-permute-start.1
  230.7 3.9 %collective-permute-start = (bf16[512,256]{1,0:T(8,128)(2,1)}, bf16[512,256]{1,0:T(8,128)(2,1)S(1)}, u32[]{:S(2)}, u32[]{:S(2)}) collective-permute-start(bf16[512,256]{1,0:T(8,128)(2,1)} %get-tuple-element.190), channel_id=1, source_target_pairs={{0,8},{8,16},{16,24},{24,32},{32,40},{40,48},{48,56},{56,64},{64,7... | collective-permute-start | bytes 786440 | tf_op jit(solution)/shard_map/while/body/eval_jaxpr/ppermute | solution.py:29
  234.6 12.3 %collective-permute-done.1 = bf16[512,256]{1,0:T(8,128)(2,1)S(1)} collective-permute-done((bf16[512,256]{1,0:T(8,128)(2,1)}, bf16[512,256]{1,0:T(8,128)(2,1)S(1)}, u32[]{:S(2)}, u32[]{:S(2)}) %collective-permute-start.1) | collective-permute-done | bytes 262176 | tf_op jit(solution)/shard_map/while/body/eval_jaxpr/ppermute | solution.py:29
  248.5 3.9 %collective-permute-done = bf16[512,256]{1,0:T(8,128)(2,1)S(1)} collective-permute-done((bf16[512,256]{1,0:T(8,128)(2,1)}, bf16[512,256]{1,0:T(8,128)(2,1)S(1)}, u32[]{:S(2)}, u32[]{:S(2)}) %collective-permute-start) | collective-permute-done | bytes 262176 | tf_op jit(solution)/shard_map/while/body/eval_jaxpr/ppermute | solution.py:29
  253.9 4.1 %fusion.14 = bf16[4096,256]{0,1:T(8,128)(2,1)} fusion(bf16[4096,256]{0,1:T(8,128)(2,1)} %get-tuple-element.124, s32[]{:T(128)S(6)} %select_n.21, bf16[4096,256]{0,1:T(8,128)(2,1)} %copy.42), kind=kLoop, calls=%fused_computation.26 | loop fusion | flops 4194304 | bytes 6291460 | tf_op jit(solution)/shard_map/add | solution.py:96
  258.0 4.4 %fusion.15 = bf16[4096,256]{1,0:T(8,128)(2,1)} fusion(bf16[4096,256]{1,0:T(8,128)(2,1)S(1)} %copy-done.1, s32[]{:T(128)S(6)} %select_n.21, bf16[4096,256]{1,0:T(8,128)(2,1)S(1)} %copy-done.2), kind=kLoop, calls=%fused_computation.27 | loop fusion | flops 4194304 | bytes 6291460 | tf_op jit(solution)/shard_map/add | solution.py:95
  262.4 1.1 fusion.64
  263.8 9.2 %fusion.4 = (f32[2,512]{1,0:T(2,128)S(1)}, f32[4608,512,2]{1,0,2:T(8,128)}) fusion(pred[512,4608]{0,1:T(8,128)(4,1)S(1)} %fusion.11, bf16[512,2,128]{0,2,1:T(8,128)(2,1)S(1)} %bitcast.115, bf16[4096,256]{1,0:T(8,128)(2,1)} %fusion.15, bf16[512,256]{1,0:T(8,128)(2,1)S(1)} %bitcast.110), kind=kOutput, calls=%fused_computation.10 | convolution fusion | flops 1224473600 | bytes 23859200 | tf_op jit(solution)/shard_map/while/body/eval_jaxpr/qgd,kd->gqk/dot_general | solution.py:55
  273.0 19.0 %fusion = (f32[2,512]{1,0:T(2,128)S(1)}, f32[2,512]{1,0:T(2,128)S(1)}, f32[4608,512,2]{1,0,2:T(8,128)}) fusion(f32[4608,512,2]{1,0,2:T(8,128)} %get-tuple-element.146, f32[2,512]{1,0:T(2,128)S(1)} %get-tuple-element.145, pred[512,4608]{0,1:T(8,128)(4,1)S(1)} %fusion.11, bf16[512,2,128]{0,2,1:T(8,128)(2,1)S(1)} %bitcast.114, ...), kind=kOutput, calls=%fused_computation.6 | convolution fusion | flops 1243346944 | bytes 42741760 | tf_op jit(solution)/shard_map/while/body/eval_jaxpr/qgd,kd->gqk/dot_general | solution.py:55
  292.0 9.8 %fusion.51 = bf16[512,2,128]{0,2,1:T(8,128)(2,1)S(1)} fusion(f32[4608,512,2]{1,0,2:T(8,128)} %get-tuple-element.146, f32[2,512]{1,0:T(2,128)S(1)} %get-tuple-element.145, pred[512,4608]{0,1:T(8,128)(4,1)S(1)} %fusion.11, bf16[4096,256]{0,1:T(8,128)(2,1)S(1)} %copy-done.3, bf16[512,256]{0,1:T(8,128)(2,1)S(1)} %copy-done.6, f32[512,2]{0,1:T(2,128)S(1)} %bitcast.117), kind=kOutput, calls=%fused_computation.45 | convolution fusion | flops 1229455360 | bytes 23863296 | tf_op jit(solution)/shard_map/while/body/eval_jaxpr/gqk,kd->qgd/dot_general | solution.py:63
  302.2 9.9 %fusion.2 = f32[2,512]{1,0:T(2,128)S(1)} fusion(f32[4608,512,2]{1,0,2:T(8,128)} %get-tuple-element.147, f32[2,512]{1,0:T(2,128)S(1)} %get-tuple-element.132, pred[512,4608]{0,1:T(8,128)(4,1)S(1)} %fusion.11), kind=kLoop, calls=%fused_computation.8 | loop fusion | flops 18873344 | bytes 21241856 | tf_op jit(solution)/shard_map/while/body/eval_jaxpr/reduce_sum | solution.py:61
  312.1 1.9 copy-done
  314.0 6.9 %fusion.41 = bf16[512,2,128]{0,2,1:T(8,128)(2,1)S(1)} fusion(f32[4608,512,2]{1,0,2:T(8,128)S(1)} %copy-done, f32[2,512]{1,0:T(2,128)S(1)} %get-tuple-element.132, pred[512,4608]{0,1:T(8,128)(4,1)S(1)} %fusion.11, bf16[512,256]{0,1:T(8,128)(2,1)S(1)} %copy-done.6, bf16[4096,256]{0,1:T(8,128)(2,1)} %fusion.14, f32[512,2]{0,1:T(2,128)S(1)} %bitcast.116), kind=kOutput, calls=%fused_computation.43 | convolution fusion | flops 1229455360 | bytes 23863296 | tf_op jit(solution)/shard_map/while/body/eval_jaxpr/gqk,kd->qgd/dot_general | solution.py:63
  321.3 69.0 %all_to_all.59 = bf16[8,64,512]{2,1,0:T(8,128)(2,1)S(1)} all-to-all(bf16[8,64,512]{2,1,0:T(8,128)(2,1)S(1)} %pad_maximum_fusion.2), channel_id=1, replica_groups=mesh['seq'=32,'head'=8] {'head'}, dimensions={0} | all-to-all | bytes 1048576 | tf_op jit(solution)/shard_map/all_to_all | solution.py:113
  390.4 0.8 copy.65
  (65 shorter events, 25.2 us)
Async XLA Ops:
  0.0 34.1 %copy-start.5 = (bf16[64,4096]{1,0:T(8,128)(2,1)S(1)}, bf16[64,4096]{1,0:T(8,128)(2,1)}, u32[]{:S(2)}) copy-start(bf16[64,4096]{1,0:T(8,128)(2,1)} %param.8) | copy-start | bytes 1572868
  11.1 15.8 %all-to-all-start.1 = ((bf16[8,64,256]{2,1,0:T(8,128)(2,1)}), bf16[8,64,256]{2,1,0:T(8,128)(2,1)}, u32[]{:S(2)}, u32[]{:S(2)}) async-start(bf16[8,64,256]{2,1,0:T(8,128)(2,1)} %bitcast_dynamic-update-slice_fusion), calls=%async_computation.1 | async-start | bytes 524288 | tf_op jit(solution)/shard_map/all_to_all | solution.py:16
  26.8 14.1 %all-to-all-start = ((bf16[64,8,256]{2,0,1:T(8,128)(2,1)}), bf16[64,8,256]{2,0,1:T(8,128)(2,1)S(1)}, u32[]{:S(2)}, u32[]{:S(2)}) async-start(bf16[64,8,256]{2,0,1:T(8,128)(2,1)} %bitcast.106), calls=%async_computation | async-start | bytes 524288 | tf_op jit(solution)/shard_map/all_to_all | solution.py:73
  40.9 221.5 %all-to-all-start.2 = ((bf16[64,8,512]{2,0,1:T(8,128)(2,1)}), bf16[64,8,512]{2,0,1:T(8,128)(2,1)}, u32[]{:S(2)}, u32[]{:S(2)}) async-start(bf16[64,8,512]{2,0,1:T(8,128)(2,1)} %bitcast.105), calls=%async_computation.2 | async-start | bytes 1048576 | tf_op jit(solution)/shard_map/all_to_all | solution.py:72
  49.6 21.0 %collective-permute-start.1 = (bf16[512,256]{1,0:T(8,128)(2,1)}, bf16[512,256]{1,0:T(8,128)(2,1)S(1)}, u32[]{:S(2)}, u32[]{:S(2)}) collective-permute-start(bf16[512,256]{1,0:T(8,128)(2,1)} %get-tuple-element.191), channel_id=1, source_target_pairs={{0,8},{8,16},{16,24},{24,32},{32,40},{40,48},{48,56},{56,64},{64,7... | collective-permute-start | bytes 786440 | tf_op jit(solution)/shard_map/while/body/eval_jaxpr/ppermute | solution.py:29
  56.7 22.2 %collective-permute-start = (bf16[512,256]{1,0:T(8,128)(2,1)}, bf16[512,256]{1,0:T(8,128)(2,1)S(1)}, u32[]{:S(2)}, u32[]{:S(2)}) collective-permute-start(bf16[512,256]{1,0:T(8,128)(2,1)} %get-tuple-element.190), channel_id=1, source_target_pairs={{0,8},{8,16},{16,24},{24,32},{32,40},{40,48},{48,56},{56,64},{64,7... | collective-permute-start | bytes 786440 | tf_op jit(solution)/shard_map/while/body/eval_jaxpr/ppermute | solution.py:29
  80.3 18.2 %collective-permute-start.1 = (bf16[512,256]{1,0:T(8,128)(2,1)}, bf16[512,256]{1,0:T(8,128)(2,1)S(1)}, u32[]{:S(2)}, u32[]{:S(2)}) collective-permute-start(bf16[512,256]{1,0:T(8,128)(2,1)} %get-tuple-element.191), channel_id=1, source_target_pairs={{0,8},{8,16},{16,24},{24,32},{32,40},{40,48},{48,56},{56,64},{64,7... | collective-permute-start | bytes 786440 | tf_op jit(solution)/shard_map/while/body/eval_jaxpr/ppermute | solution.py:29
  82.9 20.4 %collective-permute-start = (bf16[512,256]{1,0:T(8,128)(2,1)}, bf16[512,256]{1,0:T(8,128)(2,1)S(1)}, u32[]{:S(2)}, u32[]{:S(2)}) collective-permute-start(bf16[512,256]{1,0:T(8,128)(2,1)} %get-tuple-element.190), channel_id=1, source_target_pairs={{0,8},{8,16},{16,24},{24,32},{32,40},{40,48},{48,56},{56,64},{64,7... | collective-permute-start | bytes 786440 | tf_op jit(solution)/shard_map/while/body/eval_jaxpr/ppermute | solution.py:29
  104.8 18.3 %collective-permute-start.1 = (bf16[512,256]{1,0:T(8,128)(2,1)}, bf16[512,256]{1,0:T(8,128)(2,1)S(1)}, u32[]{:S(2)}, u32[]{:S(2)}) collective-permute-start(bf16[512,256]{1,0:T(8,128)(2,1)} %get-tuple-element.191), channel_id=1, source_target_pairs={{0,8},{8,16},{16,24},{24,32},{32,40},{40,48},{48,56},{56,64},{64,7... | collective-permute-start | bytes 786440 | tf_op jit(solution)/shard_map/while/body/eval_jaxpr/ppermute | solution.py:29
  106.7 20.2 %collective-permute-start = (bf16[512,256]{1,0:T(8,128)(2,1)}, bf16[512,256]{1,0:T(8,128)(2,1)S(1)}, u32[]{:S(2)}, u32[]{:S(2)}) collective-permute-start(bf16[512,256]{1,0:T(8,128)(2,1)} %get-tuple-element.190), channel_id=1, source_target_pairs={{0,8},{8,16},{16,24},{24,32},{32,40},{40,48},{48,56},{56,64},{64,7... | collective-permute-start | bytes 786440 | tf_op jit(solution)/shard_map/while/body/eval_jaxpr/ppermute | solution.py:29
  128.3 19.0 %collective-permute-start.1 = (bf16[512,256]{1,0:T(8,128)(2,1)}, bf16[512,256]{1,0:T(8,128)(2,1)S(1)}, u32[]{:S(2)}, u32[]{:S(2)}) collective-permute-start(bf16[512,256]{1,0:T(8,128)(2,1)} %get-tuple-element.191), channel_id=1, source_target_pairs={{0,8},{8,16},{16,24},{24,32},{32,40},{40,48},{48,56},{56,64},{64,7... | collective-permute-start | bytes 786440 | tf_op jit(solution)/shard_map/while/body/eval_jaxpr/ppermute | solution.py:29
  130.3 22.7 %collective-permute-start = (bf16[512,256]{1,0:T(8,128)(2,1)}, bf16[512,256]{1,0:T(8,128)(2,1)S(1)}, u32[]{:S(2)}, u32[]{:S(2)}) collective-permute-start(bf16[512,256]{1,0:T(8,128)(2,1)} %get-tuple-element.190), channel_id=1, source_target_pairs={{0,8},{8,16},{16,24},{24,32},{32,40},{40,48},{48,56},{56,64},{64,7... | collective-permute-start | bytes 786440 | tf_op jit(solution)/shard_map/while/body/eval_jaxpr/ppermute | solution.py:29
  154.4 18.2 %collective-permute-start.1 = (bf16[512,256]{1,0:T(8,128)(2,1)}, bf16[512,256]{1,0:T(8,128)(2,1)S(1)}, u32[]{:S(2)}, u32[]{:S(2)}) collective-permute-start(bf16[512,256]{1,0:T(8,128)(2,1)} %get-tuple-element.191), channel_id=1, source_target_pairs={{0,8},{8,16},{16,24},{24,32},{32,40},{40,48},{48,56},{56,64},{64,7... | collective-permute-start | bytes 786440 | tf_op jit(solution)/shard_map/while/body/eval_jaxpr/ppermute | solution.py:29
  156.3 21.1 %collective-permute-start = (bf16[512,256]{1,0:T(8,128)(2,1)}, bf16[512,256]{1,0:T(8,128)(2,1)S(1)}, u32[]{:S(2)}, u32[]{:S(2)}) collective-permute-start(bf16[512,256]{1,0:T(8,128)(2,1)} %get-tuple-element.190), channel_id=1, source_target_pairs={{0,8},{8,16},{16,24},{24,32},{32,40},{40,48},{48,56},{56,64},{64,7... | collective-permute-start | bytes 786440 | tf_op jit(solution)/shard_map/while/body/eval_jaxpr/ppermute | solution.py:29
  178.8 18.3 %collective-permute-start.1 = (bf16[512,256]{1,0:T(8,128)(2,1)}, bf16[512,256]{1,0:T(8,128)(2,1)S(1)}, u32[]{:S(2)}, u32[]{:S(2)}) collective-permute-start(bf16[512,256]{1,0:T(8,128)(2,1)} %get-tuple-element.191), channel_id=1, source_target_pairs={{0,8},{8,16},{16,24},{24,32},{32,40},{40,48},{48,56},{56,64},{64,7... | collective-permute-start | bytes 786440 | tf_op jit(solution)/shard_map/while/body/eval_jaxpr/ppermute | solution.py:29
  180.7 22.0 %collective-permute-start = (bf16[512,256]{1,0:T(8,128)(2,1)}, bf16[512,256]{1,0:T(8,128)(2,1)S(1)}, u32[]{:S(2)}, u32[]{:S(2)}) collective-permute-start(bf16[512,256]{1,0:T(8,128)(2,1)} %get-tuple-element.190), channel_id=1, source_target_pairs={{0,8},{8,16},{16,24},{24,32},{32,40},{40,48},{48,56},{56,64},{64,7... | collective-permute-start | bytes 786440 | tf_op jit(solution)/shard_map/while/body/eval_jaxpr/ppermute | solution.py:29
  204.1 18.2 %collective-permute-start.1 = (bf16[512,256]{1,0:T(8,128)(2,1)}, bf16[512,256]{1,0:T(8,128)(2,1)S(1)}, u32[]{:S(2)}, u32[]{:S(2)}) collective-permute-start(bf16[512,256]{1,0:T(8,128)(2,1)} %get-tuple-element.191), channel_id=1, source_target_pairs={{0,8},{8,16},{16,24},{24,32},{32,40},{40,48},{48,56},{56,64},{64,7... | collective-permute-start | bytes 786440 | tf_op jit(solution)/shard_map/while/body/eval_jaxpr/ppermute | solution.py:29
  206.0 21.3 %collective-permute-start = (bf16[512,256]{1,0:T(8,128)(2,1)}, bf16[512,256]{1,0:T(8,128)(2,1)S(1)}, u32[]{:S(2)}, u32[]{:S(2)}) collective-permute-start(bf16[512,256]{1,0:T(8,128)(2,1)} %get-tuple-element.190), channel_id=1, source_target_pairs={{0,8},{8,16},{16,24},{24,32},{32,40},{40,48},{48,56},{56,64},{64,7... | collective-permute-start | bytes 786440 | tf_op jit(solution)/shard_map/while/body/eval_jaxpr/ppermute | solution.py:29
  228.7 18.2 %collective-permute-start.1 = (bf16[512,256]{1,0:T(8,128)(2,1)}, bf16[512,256]{1,0:T(8,128)(2,1)S(1)}, u32[]{:S(2)}, u32[]{:S(2)}) collective-permute-start(bf16[512,256]{1,0:T(8,128)(2,1)} %get-tuple-element.191), channel_id=1, source_target_pairs={{0,8},{8,16},{16,24},{24,32},{32,40},{40,48},{48,56},{56,64},{64,7... | collective-permute-start | bytes 786440 | tf_op jit(solution)/shard_map/while/body/eval_jaxpr/ppermute | solution.py:29
  230.7 21.8 %collective-permute-start = (bf16[512,256]{1,0:T(8,128)(2,1)}, bf16[512,256]{1,0:T(8,128)(2,1)S(1)}, u32[]{:S(2)}, u32[]{:S(2)}) collective-permute-start(bf16[512,256]{1,0:T(8,128)(2,1)} %get-tuple-element.190), channel_id=1, source_target_pairs={{0,8},{8,16},{16,24},{24,32},{32,40},{40,48},{48,56},{56,64},{64,7... | collective-permute-start | bytes 786440 | tf_op jit(solution)/shard_map/while/body/eval_jaxpr/ppermute | solution.py:29
  253.9 4.1 %copy-start.1 = (bf16[4096,256]{1,0:T(8,128)(2,1)S(1)}, bf16[4096,256]{1,0:T(8,128)(2,1)}, u32[]{:S(2)}) copy-start(bf16[4096,256]{1,0:T(8,128)(2,1)} %get-tuple-element.125) | copy-start | bytes 6291460
  253.9 4.1 %copy-start.2 = (bf16[4096,256]{1,0:T(8,128)(2,1)S(1)}, bf16[4096,256]{1,0:T(8,128)(2,1)}, u32[]{:S(2)}) copy-start(bf16[4096,256]{1,0:T(8,128)(2,1)} %param.11) | copy-start | bytes 6291460
  263.8 9.3 %copy-start.4 = (bf16[4096,256]{1,0:T(8,128)(2,1)S(1)}, bf16[4096,256]{1,0:T(8,128)(2,1)}, u32[]{:S(2)}) copy-start(bf16[4096,256]{1,0:T(8,128)(2,1)} %fusion.15) | copy-start | bytes 6291460
  273.0 19.0 %copy-start.3 = (bf16[4096,256]{0,1:T(8,128)(2,1)S(1)}, bf16[4096,256]{0,1:T(8,128)(2,1)}, u32[]{:S(2)}) copy-start(bf16[4096,256]{0,1:T(8,128)(2,1)} %fusion.14) | copy-start | bytes 6291460
  273.0 19.0 %copy-start.6 = (bf16[512,256]{0,1:T(8,128)(2,1)S(1)}, bf16[512,256]{0,1:T(8,128)(2,1)}, u32[]{:S(2)}) copy-start(bf16[512,256]{0,1:T(8,128)(2,1)} %copy.44) | copy-start | bytes 786436
  302.2 11.8 %copy-start = (f32[4608,512,2]{1,0,2:T(8,128)S(1)}, f32[4608,512,2]{1,0,2:T(8,128)}, u32[]{:S(2)}) copy-start(f32[4608,512,2]{1,0,2:T(8,128)} %get-tuple-element.147) | copy-start | bytes 56623108
